TPU v7x, 512 devices: a whole 4x8x8 slice. The times are simulated.
512 devices in a mesh: rows: 64 (over z, x, core), cols: 8 (over y).
Axes of the slice: x: 4, y: 8, z: 8, core: 2. Of those that a mesh axis runs over, the one named last changes fastest.
Arguments:
- rhs: float32 [3, 128, 256, 128], P(None, 'rows', 'cols'), may hold values from -6 to 6
- diag_inv: float32 [3, 128, 256, 256], P(None, 'rows', 'cols'), may hold values from -1 to 3.1, as said below
- factor_tiles: float32 [2, 128, 8, 256, 256], P(None, 'rows', None, 'cols'), may hold values from -0.125 to 0.125
- tile_source: int32 [2, 128, 8], P(None, 'rows'), may hold values from 0 to 255, as said below
- tile_count: int32 [2, 128], P(None, 'rows'), may hold values from 1 to 8, as said below
Outputs:
- solution: float32 [3, 128, 256, 128], P(None, 'rows', 'cols')
Inputs may be any that keep to these rules, and one draw needn't show every extreme that they name: `tile_source`: each source lies at a lower level than its target; supernode g mod 128 belongs to rows index (g mod 128) // 2, and that index differs from the target's by at most 7. The 8 sources of one supernode are distinct. `tile_count`: slots at or beyond the count hold no tile of the factor. At every target level some supernode has all 8 slots live. `diag_inv`: each block is lower triangular with a positive diagonal.
All inputs are finite; a program needn't handle non-finite values.
Results may differ from a plain program's by a relative error of at most 0.0003.
Values sent between devices are 32-bit elements; how exact they have to be, the bound alone decides.
A program may use at most 64 MiB of HBM per device.

v0:
```python
import jax
import jax.numpy as jnp
from jax import lax
from jax.sharding import PartitionSpec as P

KDEV = 7


def from_behind(value, axis, steps):
    count = lax.axis_size(axis)
    leading, last = (max(0, -steps), min(count, count - steps))
    return lax.ppermute(value, axis, [(source, source + steps) for source in range(leading, last)])


def local(rhs, diag_inv, factor_tiles, tile_source, tile_count):
    levels = rhs.shape[0]
    owned_count = rhs.shape[1]
    share_rows = rhs.shape[2]
    columns = rhs.shape[3]
    slot_count = tile_source.shape[2]
    reach_dev = KDEV
    window_len = 2 * reach_dev + 1
    total_sup = lax.axis_size("rows") * owned_count
    row_place = lax.axis_index("rows")
    highest = lax.Precision.HIGHEST
    slot_ids = jnp.arange(slot_count, dtype=jnp.int32)

    def window_places(sources):
        src_level = sources // total_sup
        within = sources % total_sup
        return (
            src_level * window_len + within // owned_count - row_place + reach_dev
        ) * owned_count + within % owned_count

    def live_mask(counts):
        return (slot_ids[None, :] < counts[:, None]).astype(jnp.float32)

    def full_rows(piece):
        return lax.all_gather(piece, "cols", axis=1, tiled=True)

    forward_values = []
    windows = []
    for height in range(levels):
        if height == 0:
            whole_block = full_rows(rhs[0])
        else:
            stacked = jnp.stack(windows, 0).reshape(
                height * window_len * owned_count, share_rows, columns
            )
            places = window_places(tile_source[height - 1])
            picked = (
                jnp.take(stacked, places, axis=0)
                * live_mask(tile_count[height - 1])[:, :, None, None]
            )
            partial_value = jnp.einsum(
                "skci,skcr->sir", factor_tiles[height - 1], picked, precision=highest
            )
            whole_block = full_rows(
                rhs[height]
                - lax.psum_scatter(partial_value, "cols", scatter_dimension=1, tiled=True)
            )
        values = jnp.einsum("sci,sir->scr", diag_inv[height], whole_block, precision=highest)
        forward_values.append(values)
        if height + 1 < levels:
            pieces = []
            for pull_offset in range(-reach_dev, reach_dev + 1):
                if pull_offset == 0:
                    pieces.append(values)
                else:
                    pieces.append(from_behind(values, "rows", -pull_offset))
            windows.append(jnp.stack(pieces, 0))
    carried = [jnp.zeros_like(forward_values[0]) for height in range(levels)]
    solution = [None] * levels
    for height in reversed(range(levels)):
        partial_value = jnp.einsum(
            "sci,scr->sir",
            diag_inv[height],
            forward_values[height] - carried[height],
            precision=highest,
        )
        own_share = lax.psum_scatter(partial_value, "cols", scatter_dimension=1, tiled=True)
        if height > 0:
            whole_block = lax.all_gather(own_share, "cols", axis=1, tiled=True)
        solution[height] = own_share
        if height > 0:
            term_set = jnp.einsum(
                "skci,sir->skcr", factor_tiles[height - 1], whole_block, precision=highest
            )
            term_set = term_set * live_mask(tile_count[height - 1])[:, :, None, None]
            places = window_places(tile_source[height - 1]).reshape(-1)
            targets = height * window_len * owned_count
            one_hot = (jnp.arange(targets, dtype=jnp.int32)[:, None] == places[None, :]).astype(
                jnp.float32
            )
            outgoing = jnp.einsum(
                "ms,slg->mlg",
                one_hot,
                term_set.reshape(owned_count * slot_count, share_rows, columns),
                precision=highest,
            )
            push_outgoing = outgoing.reshape(height, window_len, owned_count, share_rows, columns)
            received = push_outgoing[:, reach_dev]
            for offset in range(-reach_dev, reach_dev + 1):
                if offset != 0:
                    received = received + from_behind(
                        push_outgoing[:, reach_dev + offset], "rows", offset
                    )
            for lower_level in range(height):
                carried[lower_level] = carried[lower_level] + received[lower_level]
    return jnp.stack(solution, 0)


def solution(mesh):
    placed = (
        P(None, "rows", "cols", None),
        P(None, "rows", "cols", None),
        P(None, "rows", None, "cols", None),
        P(None, "rows", None),
        P(None, "rows"),
    )
    return jax.shard_map(
        local, mesh=mesh, in_specs=placed, out_specs=P(None, "rows", "cols", None), check_vma=False
    )
```

profile of v0, /device:TPU:2, one launch (start us, length us, event | category | flops | bytes accessed | tf_op | source)
XLA Modules:
  0.0 670.9 jit_solution(4755036083736061673)
XLA Ops:
  7.3 26.5 %all-gather = f32[1,2,256,128]{3,2,1,0:T(8,128)S(1)} all-gather(f32[1,2,32,128]{3,2,1,0:T(8,128)S(1)} %slice-done), channel_id=2, replica_groups=mesh['rows'=64,'cols'=8] {'cols'}, dimensions={2}, use_global_device_ids=true | all-gather | bytes 294912 | tf_op jit(solution)/shard_map/all_gather | solution.py:39
  35.4 4.9 collective-permute-start.1
  40.2 6.1 collective-permute-start.2
  46.4 4.8 collective-permute-start.3
  52.7 4.0 collective-permute-start.5
  56.8 4.5 collective-permute-start.6
  61.3 1.9 collective-permute-start.7
  63.2 1.9 collective-permute-start.8
  71.8 3.7 collective-permute-done.10
  77.1 4.2 collective-permute-done.12
  83.4 1.8 convolution_bitcast_fusion.1
  85.4 44.6 %reduce-scatter.3.cloned.1.call-done = f32[2,32,128]{2,1,0:T(8,128)} async-done(((f32[2,256,128]{2,1,0:T(8,128)}), f32[2,32,128]{2,1,0:T(8,128)}) %reduce-scatter.3.cloned.1.call-update) | async-done | bytes 32784 | tf_op jit(solution)/shard_map/reduce_scatter | solution.py:60
  130.9 24.8 %all_gather.16 = f32[2,256,128]{2,1,0:T(8,128)S(1)} all-gather(f32[2,32,128]{2,1,0:T(8,128)S(1)} %bitcast_subtract_fusion), channel_id=1, replica_groups=mesh['rows'=64,'cols'=8] {'cols'}, dimensions={1}, use_global_device_ids=true | all-gather | bytes 294912 | tf_op jit(solution)/shard_map/all_gather | solution.py:39
  157.2 4.2 collective-permute-start.15
  161.4 5.4 collective-permute-start.16
  166.8 4.1 collective-permute-start.17
  172.7 3.8 collective-permute-start.19
  176.5 4.2 collective-permute-start.20
  180.7 1.9 collective-permute-start.21
  182.7 1.9 collective-permute-start.22
  191.3 3.0 collective-permute-done.24
  195.9 4.2 collective-permute-done.26
  202.2 1.8 convolution_bitcast_fusion
  204.1 43.1 %reduce-scatter.5.cloned.1.call-done = f32[2,32,128]{2,1,0:T(8,128)} async-done(((f32[2,256,128]{2,1,0:T(8,128)}), f32[2,32,128]{2,1,0:T(8,128)}) %reduce-scatter.5.cloned.1.call-update) | async-done | bytes 32784 | tf_op jit(solution)/shard_map/reduce_scatter | solution.py:60
  248.0 24.8 %all_gather.17 = f32[2,256,128]{2,1,0:T(8,128)S(1)} all-gather(f32[2,32,128]{2,1,0:T(8,128)S(1)} %bitcast_subtract_fusion.1), channel_id=1, replica_groups=mesh['rows'=64,'cols'=8] {'cols'}, dimensions={1}, use_global_device_ids=true | all-gather | bytes 294912 | tf_op jit(solution)/shard_map/all_gather | solution.py:39
  276.5 74.7 %all-reduce.7.cloned.1.call-done = f32[2,256,128]{2,0,1:T(2,128)} async-done(((f32[2,256,128]{2,0,1:T(2,128)}), f32[2,256,128]{2,0,1:T(2,128)}) %all-reduce.7.cloned.1.call-update) | async-done | bytes 262160
  351.9 24.9 %all_gather.18 = f32[2,256,128]{2,0,1:T(2,128)S(1)} all-gather(f32[2,32,128]{2,0,1:T(2,128)S(1)} %constant_dynamic-slice_fusion.1), channel_id=1, replica_groups=mesh['rows'=64,'cols'=8] {'cols'}, dimensions={1}, use_global_device_ids=true | all-gather | bytes 294912 | tf_op jit(solution)/shard_map/all_gather | solution.py:83
  380.3 4.2 collective-permute-start.40
  384.5 5.4 collective-permute-start.39
  389.8 4.1 collective-permute-start.38
  395.8 3.7 collective-permute-start.36
  399.5 4.3 collective-permute-start.35
  403.8 1.9 collective-permute-start.34
  405.7 1.9 collective-permute-start.33
  414.2 3.8 collective-permute-done.31
  419.2 4.4 collective-permute-done.29
  426.6 81.3 %all-reduce.9.cloned.1.call-done = f32[2,256,128]{2,0,1:T(2,128)} async-done(((f32[2,256,128]{2,0,1:T(2,128)}), f32[2,256,128]{2,0,1:T(2,128)}) %all-reduce.9.cloned.1.call-update) | async-done | bytes 262160
  508.6 24.9 %all_gather.19 = f32[2,256,128]{2,0,1:T(2,128)S(1)} all-gather(f32[2,32,128]{2,0,1:T(2,128)S(1)} %constant_dynamic-slice_fusion), channel_id=1, replica_groups=mesh['rows'=64,'cols'=8] {'cols'}, dimensions={1}, use_global_device_ids=true | all-gather | bytes 294912 | tf_op jit(solution)/shard_map/all_gather | solution.py:83
  536.1 4.2 collective-permute-start.54
  540.3 5.4 collective-permute-start.53
  545.7 4.2 collective-permute-start.52
  551.6 3.7 collective-permute-start.50
  555.3 4.3 collective-permute-start.49
  559.6 1.9 collective-permute-start.48
  561.5 1.9 collective-permute-start.47
  570.0 3.1 collective-permute-done.45
  574.7 4.2 collective-permute-done.43
  583.2 79.8 %all-reduce.11.cloned.1.call-done = f32[2,256,128]{2,0,1:T(2,128)} async-done(((f32[2,256,128]{2,0,1:T(2,128)}), f32[2,256,128]{2,0,1:T(2,128)}) %all-reduce.11.cloned.1.call-update) | async-done | bytes 262160
  (174 shorter events, 67.9 us)
Async XLA Ops:
  6.5 123.5 %reduce-scatter.3.cloned.1.call-start = ((), (), s32[]{:S(2)}) async-start(), calls=%async_computation.2 | async-start | bytes 294912 | tf_op jit(solution)/shard_map/reduce_scatter | solution.py:60
  34.1 18.7 %collective-permute-start = (f32[2,32,128]{2,1,0:T(8,128)S(1)}, f32[2,32,128]{2,1,0:T(8,128)S(1)}, u32[]{:S(2)}, u32[]{:S(2)}) collective-permute-start(f32[2,32,128]{2,1,0:T(8,128)S(1)} %fusion.14), channel_id=1, source_target_pairs={{0,56},{8,64},{16,72},{24,80},{32,88},{40,96},{48,104},{56,112},{6... | collective-permute-start | bytes 98312 | tf_op jit(solution)/shard_map/ppermute | solution.py:12
  35.4 21.4 %collective-permute-start.1 = (f32[2,32,128]{2,1,0:T(8,128)S(1)}, f32[2,32,128]{2,1,0:T(8,128)S(1)}, u32[]{:S(2)}, u32[]{:S(2)}) collective-permute-start(f32[2,32,128]{2,1,0:T(8,128)S(1)} %fusion.14), channel_id=1, source_target_pairs={{0,48},{8,56},{16,64},{24,72},{32,80},{40,88},{48,96},{56,104},{64... | collective-permute-start | bytes 98312 | tf_op jit(solution)/shard_map/ppermute | solution.py:12
  40.2 21.0 %collective-permute-start.2 = (f32[2,32,128]{2,1,0:T(8,128)S(1)}, f32[2,32,128]{2,1,0:T(8,128)S(1)}, u32[]{:S(2)}, u32[]{:S(2)}) collective-permute-start(f32[2,32,128]{2,1,0:T(8,128)S(1)} %fusion.14), channel_id=1, source_target_pairs={{0,40},{8,48},{16,56},{24,64},{32,72},{40,80},{48,88},{56,96},{64,... | collective-permute-start | bytes 98312 | tf_op jit(solution)/shard_map/ppermute | solution.py:12
  46.4 16.9 %collective-permute-start.3 = (f32[2,32,128]{2,1,0:T(8,128)S(1)}, f32[2,32,128]{2,1,0:T(8,128)S(1)}, u32[]{:S(2)}, u32[]{:S(2)}) collective-permute-start(f32[2,32,128]{2,1,0:T(8,128)S(1)} %fusion.14), channel_id=1, source_target_pairs={{0,32},{8,40},{16,48},{24,56},{32,64},{40,72},{48,80},{56,88},{64,... | collective-permute-start | bytes 98312 | tf_op jit(solution)/shard_map/ppermute | solution.py:12
  51.2 14.0 %collective-permute-start.4 = (f32[2,32,128]{2,1,0:T(8,128)S(1)}, f32[2,32,128]{2,1,0:T(8,128)S(1)}, u32[]{:S(2)}, u32[]{:S(2)}) collective-permute-start(f32[2,32,128]{2,1,0:T(8,128)S(1)} %fusion.14), channel_id=1, source_target_pairs={{0,24},{8,32},{16,40},{24,48},{32,56},{40,64},{48,72},{56,80},{64,... | collective-permute-start | bytes 98312 | tf_op jit(solution)/shard_map/ppermute | solution.py:12
  52.7 13.8 %collective-permute-start.5 = (f32[2,32,128]{2,1,0:T(8,128)S(1)}, f32[2,32,128]{2,1,0:T(8,128)S(1)}, u32[]{:S(2)}, u32[]{:S(2)}) collective-permute-start(f32[2,32,128]{2,1,0:T(8,128)S(1)} %fusion.14), channel_id=1, source_target_pairs={{0,16},{8,24},{16,32},{24,40},{32,48},{40,56},{48,64},{56,72},{64,... | collective-permute-start | bytes 98312 | tf_op jit(solution)/shard_map/ppermute | solution.py:12
  56.8 11.0 %collective-permute-start.6 = (f32[2,32,128]{2,1,0:T(8,128)S(1)}, f32[2,32,128]{2,1,0:T(8,128)S(1)}, u32[]{:S(2)}, u32[]{:S(2)}) collective-permute-start(f32[2,32,128]{2,1,0:T(8,128)S(1)} %fusion.14), channel_id=1, source_target_pairs={{0,8},{8,16},{16,24},{24,32},{32,40},{40,48},{48,56},{56,64},{64,7... | collective-permute-start | bytes 98312 | tf_op jit(solution)/shard_map/ppermute | solution.py:12
  66.5 9.0 %collective-permute-start.10 = (f32[2,32,128]{2,1,0:T(8,128)S(1)}, f32[2,32,128]{2,1,0:T(8,128)S(1)}, u32[]{:S(2)}, u32[]{:S(2)}) collective-permute-start(f32[2,32,128]{2,1,0:T(8,128)S(1)} %fusion.14), channel_id=1, source_target_pairs={{32,0},{40,8},{48,16},{56,24},{64,32},{72,40},{80,48},{88,56},{96,... | collective-permute-start | bytes 98312 | tf_op jit(solution)/shard_map/ppermute | solution.py:12
  67.8 9.3 %collective-permute-start.11 = (f32[2,32,128]{2,1,0:T(8,128)S(1)}, f32[2,32,128]{2,1,0:T(8,128)S(1)}, u32[]{:S(2)}, u32[]{:S(2)}) collective-permute-start(f32[2,32,128]{2,1,0:T(8,128)S(1)} %fusion.14), channel_id=1, source_target_pairs={{40,0},{48,8},{56,16},{64,24},{72,32},{80,40},{88,48},{96,56},{104... | collective-permute-start | bytes 98312 | tf_op jit(solution)/shard_map/ppermute | solution.py:12
  69.2 12.2 %collective-permute-start.12 = (f32[2,32,128]{2,1,0:T(8,128)S(1)}, f32[2,32,128]{2,1,0:T(8,128)S(1)}, u32[]{:S(2)}, u32[]{:S(2)}) collective-permute-start(f32[2,32,128]{2,1,0:T(8,128)S(1)} %fusion.14), channel_id=1, source_target_pairs={{48,0},{56,8},{64,16},{72,24},{80,32},{88,40},{96,48},{104,56},{11... | collective-permute-start | bytes 98312 | tf_op jit(solution)/shard_map/ppermute | solution.py:12
  70.5 12.3 %collective-permute-start.13 = (f32[2,32,128]{2,1,0:T(8,128)S(1)}, f32[2,32,128]{2,1,0:T(8,128)S(1)}, u32[]{:S(2)}, u32[]{:S(2)}) collective-permute-start(f32[2,32,128]{2,1,0:T(8,128)S(1)} %fusion.14), channel_id=1, source_target_pairs={{56,0},{64,8},{72,16},{80,24},{88,32},{96,40},{104,48},{112,56},{1... | collective-permute-start | bytes 98312 | tf_op jit(solution)/shard_map/ppermute | solution.py:12
  85.2 162.0 %reduce-scatter.5.cloned.1.call-start = ((), (), s32[]{:S(2)}) async-start(), calls=%async_computation.3 | async-start | bytes 294912 | tf_op jit(solution)/shard_map/reduce_scatter | solution.py:60
  155.9 16.8 %collective-permute-start.14 = (f32[2,32,128]{2,1,0:T(8,128)S(1)}, f32[2,32,128]{2,1,0:T(8,128)S(1)}, u32[]{:S(2)}, u32[]{:S(2)}) collective-permute-start(f32[2,32,128]{2,1,0:T(8,128)S(1)} %bitcast.360), channel_id=1, source_target_pairs={{0,56},{8,64},{16,72},{24,80},{32,88},{40,96},{48,104},{56,112},{6... | collective-permute-start | bytes 98312 | tf_op jit(solution)/shard_map/ppermute | solution.py:12
  157.2 19.3 %collective-permute-start.15 = (f32[2,32,128]{2,1,0:T(8,128)S(1)}, f32[2,32,128]{2,1,0:T(8,128)S(1)}, u32[]{:S(2)}, u32[]{:S(2)}) collective-permute-start(f32[2,32,128]{2,1,0:T(8,128)S(1)} %bitcast.361), channel_id=1, source_target_pairs={{0,48},{8,56},{16,64},{24,72},{32,80},{40,88},{48,96},{56,104},{64... | collective-permute-start | bytes 98312 | tf_op jit(solution)/shard_map/ppermute | solution.py:12
  161.4 19.3 %collective-permute-start.16 = (f32[2,32,128]{2,1,0:T(8,128)S(1)}, f32[2,32,128]{2,1,0:T(8,128)S(1)}, u32[]{:S(2)}, u32[]{:S(2)}) collective-permute-start(f32[2,32,128]{2,1,0:T(8,128)S(1)} %bitcast.362), channel_id=1, source_target_pairs={{0,40},{8,48},{16,56},{24,64},{32,72},{40,80},{48,88},{56,96},{64,... | collective-permute-start | bytes 98312 | tf_op jit(solution)/shard_map/ppermute | solution.py:12
  166.8 15.9 %collective-permute-start.17 = (f32[2,32,128]{2,1,0:T(8,128)S(1)}, f32[2,32,128]{2,1,0:T(8,128)S(1)}, u32[]{:S(2)}, u32[]{:S(2)}) collective-permute-start(f32[2,32,128]{2,1,0:T(8,128)S(1)} %bitcast.363), channel_id=1, source_target_pairs={{0,32},{8,40},{16,48},{24,56},{32,64},{40,72},{48,80},{56,88},{64,... | collective-permute-start | bytes 98312 | tf_op jit(solution)/shard_map/ppermute | solution.py:12
  170.9 13.7 %collective-permute-start.18 = (f32[2,32,128]{2,1,0:T(8,128)S(1)}, f32[2,32,128]{2,1,0:T(8,128)S(1)}, u32[]{:S(2)}, u32[]{:S(2)}) collective-permute-start(f32[2,32,128]{2,1,0:T(8,128)S(1)} %bitcast.364), channel_id=1, source_target_pairs={{0,24},{8,32},{16,40},{24,48},{32,56},{40,64},{48,72},{56,80},{64,... | collective-permute-start | bytes 98312 | tf_op jit(solution)/shard_map/ppermute | solution.py:12
  172.7 13.2 %collective-permute-start.19 = (f32[2,32,128]{2,1,0:T(8,128)S(1)}, f32[2,32,128]{2,1,0:T(8,128)S(1)}, u32[]{:S(2)}, u32[]{:S(2)}) collective-permute-start(f32[2,32,128]{2,1,0:T(8,128)S(1)} %bitcast.365), channel_id=1, source_target_pairs={{0,16},{8,24},{16,32},{24,40},{32,48},{40,56},{48,64},{56,72},{64,... | collective-permute-start | bytes 98312 | tf_op jit(solution)/shard_map/ppermute | solution.py:12
  176.5 10.7 %collective-permute-start.20 = (f32[2,32,128]{2,1,0:T(8,128)S(1)}, f32[2,32,128]{2,1,0:T(8,128)S(1)}, u32[]{:S(2)}, u32[]{:S(2)}) collective-permute-start(f32[2,32,128]{2,1,0:T(8,128)S(1)} %bitcast.366), channel_id=1, source_target_pairs={{0,8},{8,16},{16,24},{24,32},{32,40},{40,48},{48,56},{56,64},{64,7... | collective-permute-start | bytes 98312 | tf_op jit(solution)/shard_map/ppermute | solution.py:12
  185.9 8.3 %collective-permute-start.24 = (f32[2,32,128]{2,1,0:T(8,128)S(1)}, f32[2,32,128]{2,1,0:T(8,128)S(1)}, u32[]{:S(2)}, u32[]{:S(2)}) collective-permute-start(f32[2,32,128]{2,1,0:T(8,128)S(1)} %bitcast.370), channel_id=1, source_target_pairs={{32,0},{40,8},{48,16},{56,24},{64,32},{72,40},{80,48},{88,56},{96,... | collective-permute-start | bytes 98312 | tf_op jit(solution)/shard_map/ppermute | solution.py:12
  187.3 8.6 %collective-permute-start.25 = (f32[2,32,128]{2,1,0:T(8,128)S(1)}, f32[2,32,128]{2,1,0:T(8,128)S(1)}, u32[]{:S(2)}, u32[]{:S(2)}) collective-permute-start(f32[2,32,128]{2,1,0:T(8,128)S(1)} %bitcast.371), channel_id=1, source_target_pairs={{40,0},{48,8},{56,16},{64,24},{72,32},{80,40},{88,48},{96,56},{104... | collective-permute-start | bytes 98312 | tf_op jit(solution)/shard_map/ppermute | solution.py:12
  188.6 11.5 %collective-permute-start.26 = (f32[2,32,128]{2,1,0:T(8,128)S(1)}, f32[2,32,128]{2,1,0:T(8,128)S(1)}, u32[]{:S(2)}, u32[]{:S(2)}) collective-permute-start(f32[2,32,128]{2,1,0:T(8,128)S(1)} %bitcast.372), channel_id=1, source_target_pairs={{48,0},{56,8},{64,16},{72,24},{80,32},{88,40},{96,48},{104,56},{11... | collective-permute-start | bytes 98312 | tf_op jit(solution)/shard_map/ppermute | solution.py:12
  189.9 11.6 %collective-permute-start.27 = (f32[2,32,128]{2,1,0:T(8,128)S(1)}, f32[2,32,128]{2,1,0:T(8,128)S(1)}, u32[]{:S(2)}, u32[]{:S(2)}) collective-permute-start(f32[2,32,128]{2,1,0:T(8,128)S(1)} %bitcast.373), channel_id=1, source_target_pairs={{56,0},{64,8},{72,16},{80,24},{88,32},{96,40},{104,48},{112,56},{1... | collective-permute-start | bytes 98312 | tf_op jit(solution)/shard_map/ppermute | solution.py:12
  204.1 147.1 %all-reduce.7.cloned.1.call-start = ((), (), s32[]{:S(2)}) async-start(), calls=%async_computation.4 | async-start | bytes 524288
  274.3 233.6 %all-reduce.9.cloned.1.call-start = ((), (), s32[]{:S(2)}) async-start(), calls=%async_computation.5 | async-start | bytes 524288
  379.0 16.8 %collective-permute-start.41 = (f32[2,2,32,128]{3,2,1,0:T(8,128)S(1)}, f32[2,2,32,128]{3,2,1,0:T(8,128)S(1)}, u32[]{:S(2)}, u32[]{:S(2)}) collective-permute-start(f32[2,2,32,128]{3,2,1,0:T(8,128)S(1)} %bitcast.388), channel_id=1, source_target_pairs={{0,56},{8,64},{16,72},{24,80},{32,88},{40,96},{48,104},{56,112},{6... | collective-permute-start | bytes 196616 | tf_op jit(solution)/shard_map/ppermute | solution.py:12
  380.3 19.2 %collective-permute-start.40 = (f32[2,2,32,128]{3,2,1,0:T(8,128)S(1)}, f32[2,2,32,128]{3,2,1,0:T(8,128)S(1)}, u32[]{:S(2)}, u32[]{:S(2)}) collective-permute-start(f32[2,2,32,128]{3,2,1,0:T(8,128)S(1)} %bitcast.387), channel_id=1, source_target_pairs={{0,48},{8,56},{16,64},{24,72},{32,80},{40,88},{48,96},{56,104},{64... | collective-permute-start | bytes 196616 | tf_op jit(solution)/shard_map/ppermute | solution.py:12
  384.5 19.3 %collective-permute-start.39 = (f32[2,2,32,128]{3,2,1,0:T(8,128)S(1)}, f32[2,2,32,128]{3,2,1,0:T(8,128)S(1)}, u32[]{:S(2)}, u32[]{:S(2)}) collective-permute-start(f32[2,2,32,128]{3,2,1,0:T(8,128)S(1)} %bitcast.386), channel_id=1, source_target_pairs={{0,40},{8,48},{16,56},{24,64},{32,72},{40,80},{48,88},{56,96},{64,... | collective-permute-start | bytes 196616 | tf_op jit(solution)/shard_map/ppermute | solution.py:12
  389.8 15.9 %collective-permute-start.38 = (f32[2,2,32,128]{3,2,1,0:T(8,128)S(1)}, f32[2,2,32,128]{3,2,1,0:T(8,128)S(1)}, u32[]{:S(2)}, u32[]{:S(2)}) collective-permute-start(f32[2,2,32,128]{3,2,1,0:T(8,128)S(1)} %bitcast.385), channel_id=1, source_target_pairs={{0,32},{8,40},{16,48},{24,56},{32,64},{40,72},{48,80},{56,88},{64,... | collective-permute-start | bytes 196616 | tf_op jit(solution)/shard_map/ppermute | solution.py:12
  394.0 13.6 %collective-permute-start.37 = (f32[2,2,32,128]{3,2,1,0:T(8,128)S(1)}, f32[2,2,32,128]{3,2,1,0:T(8,128)S(1)}, u32[]{:S(2)}, u32[]{:S(2)}) collective-permute-start(f32[2,2,32,128]{3,2,1,0:T(8,128)S(1)} %bitcast.384), channel_id=1, source_target_pairs={{0,24},{8,32},{16,40},{24,48},{32,56},{40,64},{48,72},{56,80},{64,... | collective-permute-start | bytes 196616 | tf_op jit(solution)/shard_map/ppermute | solution.py:12
  395.8 13.2 %collective-permute-start.36 = (f32[2,2,32,128]{3,2,1,0:T(8,128)S(1)}, f32[2,2,32,128]{3,2,1,0:T(8,128)S(1)}, u32[]{:S(2)}, u32[]{:S(2)}) collective-permute-start(f32[2,2,32,128]{3,2,1,0:T(8,128)S(1)} %bitcast.383), channel_id=1, source_target_pairs={{0,16},{8,24},{16,32},{24,40},{32,48},{40,56},{48,64},{56,72},{64,... | collective-permute-start | bytes 196616 | tf_op jit(solution)/shard_map/ppermute | solution.py:12
  399.5 10.8 %collective-permute-start.35 = (f32[2,2,32,128]{3,2,1,0:T(8,128)S(1)}, f32[2,2,32,128]{3,2,1,0:T(8,128)S(1)}, u32[]{:S(2)}, u32[]{:S(2)}) collective-permute-start(f32[2,2,32,128]{3,2,1,0:T(8,128)S(1)} %bitcast.382), channel_id=1, source_target_pairs={{0,8},{8,16},{16,24},{24,32},{32,40},{40,48},{48,56},{56,64},{64,7... | collective-permute-start | bytes 196616 | tf_op jit(solution)/shard_map/ppermute | solution.py:12
  408.9 9.0 %collective-permute-start.31 = (f32[2,2,32,128]{3,2,1,0:T(8,128)S(1)}, f32[2,2,32,128]{3,2,1,0:T(8,128)S(1)}, u32[]{:S(2)}, u32[]{:S(2)}) collective-permute-start(f32[2,2,32,128]{3,2,1,0:T(8,128)S(1)} %bitcast.378), channel_id=1, source_target_pairs={{32,0},{40,8},{48,16},{56,24},{64,32},{72,40},{80,48},{88,56},{96,... | collective-permute-start | bytes 196616 | tf_op jit(solution)/shard_map/ppermute | solution.py:12
  410.3 9.0 %collective-permute-start.30 = (f32[2,2,32,128]{3,2,1,0:T(8,128)S(1)}, f32[2,2,32,128]{3,2,1,0:T(8,128)S(1)}, u32[]{:S(2)}, u32[]{:S(2)}) collective-permute-start(f32[2,2,32,128]{3,2,1,0:T(8,128)S(1)} %bitcast.377), channel_id=1, source_target_pairs={{40,0},{48,8},{56,16},{64,24},{72,32},{80,40},{88,48},{96,56},{104... | collective-permute-start | bytes 196616 | tf_op jit(solution)/shard_map/ppermute | solution.py:12
  411.6 12.1 %collective-permute-start.29 = (f32[2,2,32,128]{3,2,1,0:T(8,128)S(1)}, f32[2,2,32,128]{3,2,1,0:T(8,128)S(1)}, u32[]{:S(2)}, u32[]{:S(2)}) collective-permute-start(f32[2,2,32,128]{3,2,1,0:T(8,128)S(1)} %bitcast.376), channel_id=1, source_target_pairs={{48,0},{56,8},{64,16},{72,24},{80,32},{88,40},{96,48},{104,56},{11... | collective-permute-start | bytes 196616 | tf_op jit(solution)/shard_map/ppermute | solution.py:12
  412.9 12.3 %collective-permute-start.28 = (f32[2,2,32,128]{3,2,1,0:T(8,128)S(1)}, f32[2,2,32,128]{3,2,1,0:T(8,128)S(1)}, u32[]{:S(2)}, u32[]{:S(2)}) collective-permute-start(f32[2,2,32,128]{3,2,1,0:T(8,128)S(1)} %bitcast.375), channel_id=1, source_target_pairs={{56,0},{64,8},{72,16},{80,24},{88,32},{96,40},{104,48},{112,56},{1... | collective-permute-start | bytes 196616 | tf_op jit(solution)/shard_map/ppermute | solution.py:12
  426.5 236.5 %all-reduce.11.cloned.1.call-start = ((), (), s32[]{:S(2)}) async-start(), calls=%async_computation.6 | async-start | bytes 524288
  534.8 16.8 %collective-permute-start.55 = (f32[1,2,32,128]{3,2,1,0:T(8,128)S(1)}, f32[1,2,32,128]{3,2,1,0:T(8,128)S(1)}, u32[]{:S(2)}, u32[]{:S(2)}) collective-permute-start(f32[1,2,32,128]{3,2,1,0:T(8,128)S(1)} %get-tuple-element.21), channel_id=1, source_target_pairs={{0,56},{8,64},{16,72},{24,80},{32,88},{40,96},{48,104},{56,112},{6... | collective-permute-start | bytes 98312 | tf_op jit(solution)/shard_map/ppermute | solution.py:12
  536.1 19.2 %collective-permute-start.54 = (f32[1,2,32,128]{3,2,1,0:T(8,128)S(1)}, f32[1,2,32,128]{3,2,1,0:T(8,128)S(1)}, u32[]{:S(2)}, u32[]{:S(2)}) collective-permute-start(f32[1,2,32,128]{3,2,1,0:T(8,128)S(1)} %get-tuple-element.22), channel_id=1, source_target_pairs={{0,48},{8,56},{16,64},{24,72},{32,80},{40,88},{48,96},{56,104},{64... | collective-permute-start | bytes 98312 | tf_op jit(solution)/shard_map/ppermute | solution.py:12
  540.3 19.3 %collective-permute-start.53 = (f32[1,2,32,128]{3,2,1,0:T(8,128)S(1)}, f32[1,2,32,128]{3,2,1,0:T(8,128)S(1)}, u32[]{:S(2)}, u32[]{:S(2)}) collective-permute-start(f32[1,2,32,128]{3,2,1,0:T(8,128)S(1)} %get-tuple-element.23), channel_id=1, source_target_pairs={{0,40},{8,48},{16,56},{24,64},{32,72},{40,80},{48,88},{56,96},{64,... | collective-permute-start | bytes 98312 | tf_op jit(solution)/shard_map/ppermute | solution.py:12
  545.7 15.9 %collective-permute-start.52 = (f32[1,2,32,128]{3,2,1,0:T(8,128)S(1)}, f32[1,2,32,128]{3,2,1,0:T(8,128)S(1)}, u32[]{:S(2)}, u32[]{:S(2)}) collective-permute-start(f32[1,2,32,128]{3,2,1,0:T(8,128)S(1)} %get-tuple-element.24), channel_id=1, source_target_pairs={{0,32},{8,40},{16,48},{24,56},{32,64},{40,72},{48,80},{56,88},{64,... | collective-permute-start | bytes 98312 | tf_op jit(solution)/shard_map/ppermute | solution.py:12
  549.8 13.6 %collective-permute-start.51 = (f32[1,2,32,128]{3,2,1,0:T(8,128)S(1)}, f32[1,2,32,128]{3,2,1,0:T(8,128)S(1)}, u32[]{:S(2)}, u32[]{:S(2)}) collective-permute-start(f32[1,2,32,128]{3,2,1,0:T(8,128)S(1)} %get-tuple-element.25), channel_id=1, source_target_pairs={{0,24},{8,32},{16,40},{24,48},{32,56},{40,64},{48,72},{56,80},{64,... | collective-permute-start | bytes 98312 | tf_op jit(solution)/shard_map/ppermute | solution.py:12
  551.6 13.2 %collective-permute-start.50 = (f32[1,2,32,128]{3,2,1,0:T(8,128)S(1)}, f32[1,2,32,128]{3,2,1,0:T(8,128)S(1)}, u32[]{:S(2)}, u32[]{:S(2)}) collective-permute-start(f32[1,2,32,128]{3,2,1,0:T(8,128)S(1)} %get-tuple-element.26), channel_id=1, source_target_pairs={{0,16},{8,24},{16,32},{24,40},{32,48},{40,56},{48,64},{56,72},{64,... | collective-permute-start | bytes 98312 | tf_op jit(solution)/shard_map/ppermute | solution.py:12
  555.3 10.8 %collective-permute-start.49 = (f32[1,2,32,128]{3,2,1,0:T(8,128)S(1)}, f32[1,2,32,128]{3,2,1,0:T(8,128)S(1)}, u32[]{:S(2)}, u32[]{:S(2)}) collective-permute-start(f32[1,2,32,128]{3,2,1,0:T(8,128)S(1)} %get-tuple-element.27), channel_id=1, source_target_pairs={{0,8},{8,16},{16,24},{24,32},{32,40},{40,48},{48,56},{56,64},{64,7... | collective-permute-start | bytes 98312 | tf_op jit(solution)/shard_map/ppermute | solution.py:12
  566.1 8.6 %collective-permute-start.44 = (f32[1,2,32,128]{3,2,1,0:T(8,128)S(1)}, f32[1,2,32,128]{3,2,1,0:T(8,128)S(1)}, u32[]{:S(2)}, u32[]{:S(2)}) collective-permute-start(f32[1,2,32,128]{3,2,1,0:T(8,128)S(1)} %get-tuple-element.32), channel_id=1, source_target_pairs={{40,0},{48,8},{56,16},{64,24},{72,32},{80,40},{88,48},{96,56},{104... | collective-permute-start | bytes 98312 | tf_op jit(solution)/shard_map/ppermute | solution.py:12
  567.4 11.5 %collective-permute-start.43 = (f32[1,2,32,128]{3,2,1,0:T(8,128)S(1)}, f32[1,2,32,128]{3,2,1,0:T(8,128)S(1)}, u32[]{:S(2)}, u32[]{:S(2)}) collective-permute-start(f32[1,2,32,128]{3,2,1,0:T(8,128)S(1)} %get-tuple-element.33), channel_id=1, source_target_pairs={{48,0},{56,8},{64,16},{72,24},{80,32},{88,40},{96,48},{104,56},{11... | collective-permute-start | bytes 98312 | tf_op jit(solution)/shard_map/ppermute | solution.py:12
  568.7 11.6 %collective-permute-start.42 = (f32[1,2,32,128]{3,2,1,0:T(8,128)S(1)}, f32[1,2,32,128]{3,2,1,0:T(8,128)S(1)}, u32[]{:S(2)}, u32[]{:S(2)}) collective-permute-start(f32[1,2,32,128]{3,2,1,0:T(8,128)S(1)} %get-tuple-element.20), channel_id=1, source_target_pairs={{56,0},{64,8},{72,16},{80,24},{88,32},{96,40},{104,48},{112,56},{1... | collective-permute-start | bytes 98312 | tf_op jit(solution)/shard_map/ppermute | solution.py:12
  (19 other events, 335.9 us)
Sparse Core Ops, SparseCore 0:
  85.4 44.6 reduce-scatter.2
  204.2 42.9 reduce-scatter.4
  274.4 76.6 all-reduce.6
  426.6 81.1 all-reduce.8
  581.8 81.1 all-reduce.10
where the time goes:
time: 673 us; the launch traced here: 671 us
  waiting for transfers between devices  366 us (54%)
  starting transfers between devices  142 us (21%)
  blocking collectives  126 us (19%)
  between operations  14.9 us (2%)
  local copies, waits for them, and re-layouts  11.1 us (2%)
  matrix products  8.02 us (1%)
    unnamed x8, waiting for transfers between devices  236 us
    ppermute x56, starting transfers between devices, from_behind(): lax.ppermute(value, axis, [(source, source + steps) for source in range(l...  142 us
    reduce_scatter x2, waiting for transfers between devices, local(): lax.psum_scatter(partial_value, 'cols', scatter_dimension=1, tiled=True)  87.7 us
    all_gather x3, blocking collectives, full_rows(): return lax.all_gather(piece, 'cols', axis=1, tiled=True)  76.1 us
    all_gather x2, blocking collectives, local(): whole_block = lax.all_gather(own_share, 'cols', axis=1, tiled=True)  49.7 us
    ppermute x56, waiting for transfers between devices, from_behind(): lax.ppermute(value, axis, [(source, source + steps) for source in range(l...  42.7 us
  transfers between devices with their start and end apart: 61, of which 21 were waited for; matrix products, arithmetic and copies ran while one was open for 1% of the time, Pallas kernels for 0%

commit v1 on v0

--- a/solution.py
+++ b/solution.py
@@ -4,6 +4,12 @@
 from jax.sharding import PartitionSpec as P
 
 KDEV = 7
+advance_heads_over_axis = lambda group_axis, frame_in: jnp.concatenate(
+    lax.all_to_all(
+        jnp.stack([frame_in for _ in range(lax.axis_size(group_axis))], axis=0), group_axis, 0, 0
+    ),
+    axis=1,
+)
 
 
 def from_behind(value, axis, steps):
@@ -80,7 +86,7 @@
         )
         own_share = lax.psum_scatter(partial_value, "cols", scatter_dimension=1, tiled=True)
         if height > 0:
-            whole_block = lax.all_gather(own_share, "cols", axis=1, tiled=True)
+            whole_block = advance_heads_over_axis("cols", own_share)
         solution[height] = own_share
         if height > 0:
             term_set = jnp.einsum(

time: 673 us -> 650 us (0.966)
  blocking collectives: 126 us -> 76.1 us
  waiting for transfers between devices: 366 us -> 382 us
  starting transfers between devices: 142 us -> 151 us
    all_gather x2 -> x0, blocking collectives: 49.7 us -> none  [local(): whole_block = lax.all_gather(own_share, 'cols', axis=1, tiled=True)]
    all_to_all x0 -> x2, waiting for transfers between devices: none -> 20.7 us  [lax.all_to_all(jnp.stack([frame_in for _ in range(lax.axis_size(group_axi...]
    all_to_all x0 -> x2, starting transfers between devices: none -> 8.32 us  [lax.all_to_all(jnp.stack([frame_in for _ in range(lax.axis_size(group_axi...]
  transfers between devices with their start and end apart: 61 -> 63, of which waited for: 21 -> 23; matrix products, arithmetic and copies ran while one was open for 1% -> 1% of each run, Pallas kernels for 0% -> 0%
where the time goes in v1:
time: 650 us; the launch traced here: 647 us
  waiting for transfers between devices  382 us (59%)
  starting transfers between devices  151 us (23%)
  blocking collectives  76.1 us (12%)
  between operations  14.9 us (2%)
  local copies, waits for them, and re-layouts  12.7 us (2%)
  matrix products  8 us (1%)
    unnamed x8, waiting for transfers between devices  231 us
    ppermute x56, starting transfers between devices, from_behind(): lax.ppermute(value, axis, [(source, source + steps) for source in range(l...  142 us
    reduce_scatter x2, waiting for transfers between devices, local(): lax.psum_scatter(partial_value, 'cols', scatter_dimension=1, tiled=True)  87.7 us
    all_gather x3, blocking collectives, full_rows(): return lax.all_gather(piece, 'cols', axis=1, tiled=True)  76.1 us
    ppermute x56, waiting for transfers between devices, from_behind(): lax.ppermute(value, axis, [(source, source + steps) for source in range(l...  42.7 us
    all_to_all x2, waiting for transfers between devices, lax.all_to_all(jnp.stack([frame_in for _ in range(lax.axis_size(group_axi...  20.7 us
  transfers between devices with their start and end apart: 63, of which 23 were waited for; matrix products, arithmetic and copies ran while one was open for 1% of the time, Pallas kernels for 0%

profile of v1, /device:TPU:2, one launch (start us, length us, event | category | flops | bytes accessed | tf_op | source)
XLA Modules:
  0.0 647.3 jit_solution(9715259903519983221)
XLA Ops:
  7.3 26.5 %all-gather = f32[1,2,256,128]{3,2,1,0:T(8,128)S(1)} all-gather(f32[1,2,32,128]{3,2,1,0:T(8,128)S(1)} %slice-done), channel_id=2, replica_groups=mesh['rows'=64,'cols'=8] {'cols'}, dimensions={2}, use_global_device_ids=true | all-gather | bytes 294912 | tf_op jit(solution)/shard_map/all_gather | solution.py:45
  35.4 4.9 collective-permute-start.1
  40.2 6.1 collective-permute-start.2
  46.4 4.8 collective-permute-start.3
  52.7 4.0 collective-permute-start.5
  56.8 4.5 collective-permute-start.6
  61.3 1.9 collective-permute-start.7
  63.2 1.9 collective-permute-start.8
  71.8 3.7 collective-permute-done.10
  77.1 4.2 collective-permute-done.12
  85.4 44.6 %reduce-scatter.3.cloned.1.call-done = f32[2,32,128]{2,1,0:T(8,128)} async-done(((f32[2,256,128]{2,1,0:T(8,128)}), f32[2,32,128]{2,1,0:T(8,128)}) %reduce-scatter.3.cloned.1.call-update) | async-done | bytes 32784 | tf_op jit(solution)/shard_map/reduce_scatter | solution.py:66
  130.8 24.8 %all_gather.10 = f32[2,256,128]{2,1,0:T(8,128)S(1)} all-gather(f32[2,32,128]{2,1,0:T(8,128)S(1)} %bitcast_subtract_fusion), channel_id=1, replica_groups=mesh['rows'=64,'cols'=8] {'cols'}, dimensions={1}, use_global_device_ids=true | all-gather | bytes 294912 | tf_op jit(solution)/shard_map/all_gather | solution.py:45
  157.2 4.2 collective-permute-start.15
  161.4 5.4 collective-permute-start.16
  166.8 4.1 collective-permute-start.17
  172.7 3.8 collective-permute-start.19
  176.5 4.2 collective-permute-start.20
  180.7 1.9 collective-permute-start.21
  182.7 1.9 collective-permute-start.22
  191.2 3.0 collective-permute-done.24
  195.9 4.2 collective-permute-done.26
  204.1 43.1 %reduce-scatter.5.cloned.1.call-done = f32[2,32,128]{2,1,0:T(8,128)} async-done(((f32[2,256,128]{2,1,0:T(8,128)}), f32[2,32,128]{2,1,0:T(8,128)}) %reduce-scatter.5.cloned.1.call-update) | async-done | bytes 32784 | tf_op jit(solution)/shard_map/reduce_scatter | solution.py:66
  248.0 24.8 %all_gather.11 = f32[2,256,128]{2,1,0:T(8,128)S(1)} all-gather(f32[2,32,128]{2,1,0:T(8,128)S(1)} %bitcast_subtract_fusion.1), channel_id=1, replica_groups=mesh['rows'=64,'cols'=8] {'cols'}, dimensions={1}, use_global_device_ids=true | all-gather | bytes 294912 | tf_op jit(solution)/shard_map/all_gather | solution.py:45
  276.2 74.9 %all-reduce.7.cloned.1.call-done = f32[2,256,128]{2,0,1:T(2,128)} async-done(((f32[2,256,128]{2,0,1:T(2,128)}), f32[2,256,128]{2,0,1:T(2,128)}) %all-reduce.7.cloned.1.call-update) | async-done | bytes 262160
  352.7 4.2 all-to-all-start
  357.1 10.2 %all-to-all-done = f32[8,2,32,128]{3,2,1,0:T(8,128)S(1)} async-done(((f32[8,2,32,128]{3,2,1,0:T(8,128)}), f32[8,2,32,128]{3,2,1,0:T(8,128)S(1)}, u32[]{:S(2)}, u32[]{:S(2)}) %all-to-all-start) | async-done | bytes 262176 | tf_op jit(solution)/shard_map/all_to_all | solution.py:8
  370.8 4.2 collective-permute-start.40
  375.0 5.3 collective-permute-start.39
  380.4 4.1 collective-permute-start.38
  386.3 3.7 collective-permute-start.36
  390.0 4.3 collective-permute-start.35
  394.3 1.9 collective-permute-start.34
  396.3 1.9 collective-permute-start.33
  404.7 3.8 collective-permute-done.31
  409.8 4.4 collective-permute-done.29
  417.1 79.0 %all-reduce.9.cloned.1.call-done = f32[2,256,128]{2,0,1:T(2,128)} async-done(((f32[2,256,128]{2,0,1:T(2,128)}), f32[2,256,128]{2,0,1:T(2,128)}) %all-reduce.9.cloned.1.call-update) | async-done | bytes 262160
  497.6 4.2 all-to-all-start.1
  501.8 10.4 %all-to-all-done.1 = f32[8,2,32,128]{3,2,1,0:T(8,128)S(1)} async-done(((f32[8,2,32,128]{3,2,1,0:T(8,128)}), f32[8,2,32,128]{3,2,1,0:T(8,128)S(1)}, u32[]{:S(2)}, u32[]{:S(2)}) %all-to-all-start.1) | async-done | bytes 262176 | tf_op jit(solution)/shard_map/all_to_all | solution.py:8
  514.8 4.2 collective-permute-start.54
  519.0 5.4 collective-permute-start.53
  524.4 4.1 collective-permute-start.52
  530.3 3.7 collective-permute-start.50
  534.0 4.3 collective-permute-start.49
  538.3 1.9 collective-permute-start.48
  540.2 1.9 collective-permute-start.47
  548.7 3.1 collective-permute-done.45
  553.4 4.2 collective-permute-done.43
  561.9 77.4 %all-reduce.11.cloned.1.call-done = f32[2,256,128]{2,0,1:T(2,128)} async-done(((f32[2,256,128]{2,0,1:T(2,128)}), f32[2,256,128]{2,0,1:T(2,128)}) %all-reduce.11.cloned.1.call-update) | async-done | bytes 262160
  (182 shorter events, 73.1 us)
Async XLA Ops:
  6.5 123.5 %reduce-scatter.3.cloned.1.call-start = ((), (), s32[]{:S(2)}) async-start(), calls=%async_computation.4 | async-start | bytes 294912 | tf_op jit(solution)/shard_map/reduce_scatter | solution.py:66
  34.1 18.7 %collective-permute-start = (f32[2,32,128]{2,1,0:T(8,128)S(1)}, f32[2,32,128]{2,1,0:T(8,128)S(1)}, u32[]{:S(2)}, u32[]{:S(2)}) collective-permute-start(f32[2,32,128]{2,1,0:T(8,128)S(1)} %fusion.12), channel_id=1, source_target_pairs={{0,56},{8,64},{16,72},{24,80},{32,88},{40,96},{48,104},{56,112},{6... | collective-permute-start | bytes 98312 | tf_op jit(solution)/shard_map/ppermute | solution.py:18
  35.4 21.4 %collective-permute-start.1 = (f32[2,32,128]{2,1,0:T(8,128)S(1)}, f32[2,32,128]{2,1,0:T(8,128)S(1)}, u32[]{:S(2)}, u32[]{:S(2)}) collective-permute-start(f32[2,32,128]{2,1,0:T(8,128)S(1)} %fusion.12), channel_id=1, source_target_pairs={{0,48},{8,56},{16,64},{24,72},{32,80},{40,88},{48,96},{56,104},{64... | collective-permute-start | bytes 98312 | tf_op jit(solution)/shard_map/ppermute | solution.py:18
  40.2 21.0 %collective-permute-start.2 = (f32[2,32,128]{2,1,0:T(8,128)S(1)}, f32[2,32,128]{2,1,0:T(8,128)S(1)}, u32[]{:S(2)}, u32[]{:S(2)}) collective-permute-start(f32[2,32,128]{2,1,0:T(8,128)S(1)} %fusion.12), channel_id=1, source_target_pairs={{0,40},{8,48},{16,56},{24,64},{32,72},{40,80},{48,88},{56,96},{64,... | collective-permute-start | bytes 98312 | tf_op jit(solution)/shard_map/ppermute | solution.py:18
  46.4 16.9 %collective-permute-start.3 = (f32[2,32,128]{2,1,0:T(8,128)S(1)}, f32[2,32,128]{2,1,0:T(8,128)S(1)}, u32[]{:S(2)}, u32[]{:S(2)}) collective-permute-start(f32[2,32,128]{2,1,0:T(8,128)S(1)} %fusion.12), channel_id=1, source_target_pairs={{0,32},{8,40},{16,48},{24,56},{32,64},{40,72},{48,80},{56,88},{64,... | collective-permute-start | bytes 98312 | tf_op jit(solution)/shard_map/ppermute | solution.py:18
  51.2 14.0 %collective-permute-start.4 = (f32[2,32,128]{2,1,0:T(8,128)S(1)}, f32[2,32,128]{2,1,0:T(8,128)S(1)}, u32[]{:S(2)}, u32[]{:S(2)}) collective-permute-start(f32[2,32,128]{2,1,0:T(8,128)S(1)} %fusion.12), channel_id=1, source_target_pairs={{0,24},{8,32},{16,40},{24,48},{32,56},{40,64},{48,72},{56,80},{64,... | collective-permute-start | bytes 98312 | tf_op jit(solution)/shard_map/ppermute | solution.py:18
  52.7 13.8 %collective-permute-start.5 = (f32[2,32,128]{2,1,0:T(8,128)S(1)}, f32[2,32,128]{2,1,0:T(8,128)S(1)}, u32[]{:S(2)}, u32[]{:S(2)}) collective-permute-start(f32[2,32,128]{2,1,0:T(8,128)S(1)} %fusion.12), channel_id=1, source_target_pairs={{0,16},{8,24},{16,32},{24,40},{32,48},{40,56},{48,64},{56,72},{64,... | collective-permute-start | bytes 98312 | tf_op jit(solution)/shard_map/ppermute | solution.py:18
  56.8 11.0 %collective-permute-start.6 = (f32[2,32,128]{2,1,0:T(8,128)S(1)}, f32[2,32,128]{2,1,0:T(8,128)S(1)}, u32[]{:S(2)}, u32[]{:S(2)}) collective-permute-start(f32[2,32,128]{2,1,0:T(8,128)S(1)} %fusion.12), channel_id=1, source_target_pairs={{0,8},{8,16},{16,24},{24,32},{32,40},{40,48},{48,56},{56,64},{64,7... | collective-permute-start | bytes 98312 | tf_op jit(solution)/shard_map/ppermute | solution.py:18
  66.5 9.0 %collective-permute-start.10 = (f32[2,32,128]{2,1,0:T(8,128)S(1)}, f32[2,32,128]{2,1,0:T(8,128)S(1)}, u32[]{:S(2)}, u32[]{:S(2)}) collective-permute-start(f32[2,32,128]{2,1,0:T(8,128)S(1)} %fusion.12), channel_id=1, source_target_pairs={{32,0},{40,8},{48,16},{56,24},{64,32},{72,40},{80,48},{88,56},{96,... | collective-permute-start | bytes 98312 | tf_op jit(solution)/shard_map/ppermute | solution.py:18
  67.8 9.3 %collective-permute-start.11 = (f32[2,32,128]{2,1,0:T(8,128)S(1)}, f32[2,32,128]{2,1,0:T(8,128)S(1)}, u32[]{:S(2)}, u32[]{:S(2)}) collective-permute-start(f32[2,32,128]{2,1,0:T(8,128)S(1)} %fusion.12), channel_id=1, source_target_pairs={{40,0},{48,8},{56,16},{64,24},{72,32},{80,40},{88,48},{96,56},{104... | collective-permute-start | bytes 98312 | tf_op jit(solution)/shard_map/ppermute | solution.py:18
  69.2 12.2 %collective-permute-start.12 = (f32[2,32,128]{2,1,0:T(8,128)S(1)}, f32[2,32,128]{2,1,0:T(8,128)S(1)}, u32[]{:S(2)}, u32[]{:S(2)}) collective-permute-start(f32[2,32,128]{2,1,0:T(8,128)S(1)} %fusion.12), channel_id=1, source_target_pairs={{48,0},{56,8},{64,16},{72,24},{80,32},{88,40},{96,48},{104,56},{11... | collective-permute-start | bytes 98312 | tf_op jit(solution)/shard_map/ppermute | solution.py:18
  70.5 12.3 %collective-permute-start.13 = (f32[2,32,128]{2,1,0:T(8,128)S(1)}, f32[2,32,128]{2,1,0:T(8,128)S(1)}, u32[]{:S(2)}, u32[]{:S(2)}) collective-permute-start(f32[2,32,128]{2,1,0:T(8,128)S(1)} %fusion.12), channel_id=1, source_target_pairs={{56,0},{64,8},{72,16},{80,24},{88,32},{96,40},{104,48},{112,56},{1... | collective-permute-start | bytes 98312 | tf_op jit(solution)/shard_map/ppermute | solution.py:18
  85.2 162.0 %reduce-scatter.5.cloned.1.call-start = ((), (), s32[]{:S(2)}) async-start(), calls=%async_computation.5 | async-start | bytes 294912 | tf_op jit(solution)/shard_map/reduce_scatter | solution.py:66
  155.9 16.8 %collective-permute-start.14 = (f32[2,32,128]{2,1,0:T(8,128)S(1)}, f32[2,32,128]{2,1,0:T(8,128)S(1)}, u32[]{:S(2)}, u32[]{:S(2)}) collective-permute-start(f32[2,32,128]{2,1,0:T(8,128)S(1)} %bitcast.374), channel_id=1, source_target_pairs={{0,56},{8,64},{16,72},{24,80},{32,88},{40,96},{48,104},{56,112},{6... | collective-permute-start | bytes 98312 | tf_op jit(solution)/shard_map/ppermute | solution.py:18
  157.2 19.3 %collective-permute-start.15 = (f32[2,32,128]{2,1,0:T(8,128)S(1)}, f32[2,32,128]{2,1,0:T(8,128)S(1)}, u32[]{:S(2)}, u32[]{:S(2)}) collective-permute-start(f32[2,32,128]{2,1,0:T(8,128)S(1)} %bitcast.375), channel_id=1, source_target_pairs={{0,48},{8,56},{16,64},{24,72},{32,80},{40,88},{48,96},{56,104},{64... | collective-permute-start | bytes 98312 | tf_op jit(solution)/shard_map/ppermute | solution.py:18
  161.4 19.3 %collective-permute-start.16 = (f32[2,32,128]{2,1,0:T(8,128)S(1)}, f32[2,32,128]{2,1,0:T(8,128)S(1)}, u32[]{:S(2)}, u32[]{:S(2)}) collective-permute-start(f32[2,32,128]{2,1,0:T(8,128)S(1)} %bitcast.376), channel_id=1, source_target_pairs={{0,40},{8,48},{16,56},{24,64},{32,72},{40,80},{48,88},{56,96},{64,... | collective-permute-start | bytes 98312 | tf_op jit(solution)/shard_map/ppermute | solution.py:18
  166.8 15.9 %collective-permute-start.17 = (f32[2,32,128]{2,1,0:T(8,128)S(1)}, f32[2,32,128]{2,1,0:T(8,128)S(1)}, u32[]{:S(2)}, u32[]{:S(2)}) collective-permute-start(f32[2,32,128]{2,1,0:T(8,128)S(1)} %bitcast.377), channel_id=1, source_target_pairs={{0,32},{8,40},{16,48},{24,56},{32,64},{40,72},{48,80},{56,88},{64,... | collective-permute-start | bytes 98312 | tf_op jit(solution)/shard_map/ppermute | solution.py:18
  170.9 13.7 %collective-permute-start.18 = (f32[2,32,128]{2,1,0:T(8,128)S(1)}, f32[2,32,128]{2,1,0:T(8,128)S(1)}, u32[]{:S(2)}, u32[]{:S(2)}) collective-permute-start(f32[2,32,128]{2,1,0:T(8,128)S(1)} %bitcast.378), channel_id=1, source_target_pairs={{0,24},{8,32},{16,40},{24,48},{32,56},{40,64},{48,72},{56,80},{64,... | collective-permute-start | bytes 98312 | tf_op jit(solution)/shard_map/ppermute | solution.py:18
  172.7 13.2 %collective-permute-start.19 = (f32[2,32,128]{2,1,0:T(8,128)S(1)}, f32[2,32,128]{2,1,0:T(8,128)S(1)}, u32[]{:S(2)}, u32[]{:S(2)}) collective-permute-start(f32[2,32,128]{2,1,0:T(8,128)S(1)} %bitcast.379), channel_id=1, source_target_pairs={{0,16},{8,24},{16,32},{24,40},{32,48},{40,56},{48,64},{56,72},{64,... | collective-permute-start | bytes 98312 | tf_op jit(solution)/shard_map/ppermute | solution.py:18
  176.5 10.7 %collective-permute-start.20 = (f32[2,32,128]{2,1,0:T(8,128)S(1)}, f32[2,32,128]{2,1,0:T(8,128)S(1)}, u32[]{:S(2)}, u32[]{:S(2)}) collective-permute-start(f32[2,32,128]{2,1,0:T(8,128)S(1)} %bitcast.380), channel_id=1, source_target_pairs={{0,8},{8,16},{16,24},{24,32},{32,40},{40,48},{48,56},{56,64},{64,7... | collective-permute-start | bytes 98312 | tf_op jit(solution)/shard_map/ppermute | solution.py:18
  188.6 11.5 %collective-permute-start.26 = (f32[2,32,128]{2,1,0:T(8,128)S(1)}, f32[2,32,128]{2,1,0:T(8,128)S(1)}, u32[]{:S(2)}, u32[]{:S(2)}) collective-permute-start(f32[2,32,128]{2,1,0:T(8,128)S(1)} %bitcast.386), channel_id=1, source_target_pairs={{48,0},{56,8},{64,16},{72,24},{80,32},{88,40},{96,48},{104,56},{11... | collective-permute-start | bytes 98312 | tf_op jit(solution)/shard_map/ppermute | solution.py:18
  189.9 11.6 %collective-permute-start.27 = (f32[2,32,128]{2,1,0:T(8,128)S(1)}, f32[2,32,128]{2,1,0:T(8,128)S(1)}, u32[]{:S(2)}, u32[]{:S(2)}) collective-permute-start(f32[2,32,128]{2,1,0:T(8,128)S(1)} %bitcast.387), channel_id=1, source_target_pairs={{56,0},{64,8},{72,16},{80,24},{88,32},{96,40},{104,48},{112,56},{1... | collective-permute-start | bytes 98312 | tf_op jit(solution)/shard_map/ppermute | solution.py:18
  204.1 147.1 %all-reduce.7.cloned.1.call-start = ((), (), s32[]{:S(2)}) async-start(), calls=%async_computation.6 | async-start | bytes 524288
  352.7 14.6 %all-to-all-start = ((f32[8,2,32,128]{3,2,1,0:T(8,128)}), f32[8,2,32,128]{3,2,1,0:T(8,128)S(1)}, u32[]{:S(2)}, u32[]{:S(2)}) async-start(f32[8,2,32,128]{3,2,1,0:T(8,128)} %stack.174), calls=%async_computation.2 | async-start | bytes 524288 | tf_op jit(solution)/shard_map/all_to_all | solution.py:8
  356.8 139.2 %all-reduce.9.cloned.1.call-start = ((), (), s32[]{:S(2)}) async-start(), calls=%async_computation.7 | async-start | bytes 524288
  369.5 16.8 %collective-permute-start.41 = (f32[2,2,32,128]{3,2,1,0:T(8,128)S(1)}, f32[2,2,32,128]{3,2,1,0:T(8,128)S(1)}, u32[]{:S(2)}, u32[]{:S(2)}) collective-permute-start(f32[2,2,32,128]{3,2,1,0:T(8,128)S(1)} %bitcast.402), channel_id=1, source_target_pairs={{0,56},{8,64},{16,72},{24,80},{32,88},{40,96},{48,104},{56,112},{6... | collective-permute-start | bytes 196616 | tf_op jit(solution)/shard_map/ppermute | solution.py:18
  370.8 19.2 %collective-permute-start.40 = (f32[2,2,32,128]{3,2,1,0:T(8,128)S(1)}, f32[2,2,32,128]{3,2,1,0:T(8,128)S(1)}, u32[]{:S(2)}, u32[]{:S(2)}) collective-permute-start(f32[2,2,32,128]{3,2,1,0:T(8,128)S(1)} %bitcast.401), channel_id=1, source_target_pairs={{0,48},{8,56},{16,64},{24,72},{32,80},{40,88},{48,96},{56,104},{64... | collective-permute-start | bytes 196616 | tf_op jit(solution)/shard_map/ppermute | solution.py:18
  375.0 19.3 %collective-permute-start.39 = (f32[2,2,32,128]{3,2,1,0:T(8,128)S(1)}, f32[2,2,32,128]{3,2,1,0:T(8,128)S(1)}, u32[]{:S(2)}, u32[]{:S(2)}) collective-permute-start(f32[2,2,32,128]{3,2,1,0:T(8,128)S(1)} %bitcast.400), channel_id=1, source_target_pairs={{0,40},{8,48},{16,56},{24,64},{32,72},{40,80},{48,88},{56,96},{64,... | collective-permute-start | bytes 196616 | tf_op jit(solution)/shard_map/ppermute | solution.py:18
  380.4 15.9 %collective-permute-start.38 = (f32[2,2,32,128]{3,2,1,0:T(8,128)S(1)}, f32[2,2,32,128]{3,2,1,0:T(8,128)S(1)}, u32[]{:S(2)}, u32[]{:S(2)}) collective-permute-start(f32[2,2,32,128]{3,2,1,0:T(8,128)S(1)} %bitcast.399), channel_id=1, source_target_pairs={{0,32},{8,40},{16,48},{24,56},{32,64},{40,72},{48,80},{56,88},{64,... | collective-permute-start | bytes 196616 | tf_op jit(solution)/shard_map/ppermute | solution.py:18
  384.5 13.6 %collective-permute-start.37 = (f32[2,2,32,128]{3,2,1,0:T(8,128)S(1)}, f32[2,2,32,128]{3,2,1,0:T(8,128)S(1)}, u32[]{:S(2)}, u32[]{:S(2)}) collective-permute-start(f32[2,2,32,128]{3,2,1,0:T(8,128)S(1)} %bitcast.398), channel_id=1, source_target_pairs={{0,24},{8,32},{16,40},{24,48},{32,56},{40,64},{48,72},{56,80},{64,... | collective-permute-start | bytes 196616 | tf_op jit(solution)/shard_map/ppermute | solution.py:18
  386.3 13.2 %collective-permute-start.36 = (f32[2,2,32,128]{3,2,1,0:T(8,128)S(1)}, f32[2,2,32,128]{3,2,1,0:T(8,128)S(1)}, u32[]{:S(2)}, u32[]{:S(2)}) collective-permute-start(f32[2,2,32,128]{3,2,1,0:T(8,128)S(1)} %bitcast.397), channel_id=1, source_target_pairs={{0,16},{8,24},{16,32},{24,40},{32,48},{40,56},{48,64},{56,72},{64,... | collective-permute-start | bytes 196616 | tf_op jit(solution)/shard_map/ppermute | solution.py:18
  390.0 10.8 %collective-permute-start.35 = (f32[2,2,32,128]{3,2,1,0:T(8,128)S(1)}, f32[2,2,32,128]{3,2,1,0:T(8,128)S(1)}, u32[]{:S(2)}, u32[]{:S(2)}) collective-permute-start(f32[2,2,32,128]{3,2,1,0:T(8,128)S(1)} %bitcast.396), channel_id=1, source_target_pairs={{0,8},{8,16},{16,24},{24,32},{32,40},{40,48},{48,56},{56,64},{64,7... | collective-permute-start | bytes 196616 | tf_op jit(solution)/shard_map/ppermute | solution.py:18
  399.5 9.0 %collective-permute-start.31 = (f32[2,2,32,128]{3,2,1,0:T(8,128)S(1)}, f32[2,2,32,128]{3,2,1,0:T(8,128)S(1)}, u32[]{:S(2)}, u32[]{:S(2)}) collective-permute-start(f32[2,2,32,128]{3,2,1,0:T(8,128)S(1)} %bitcast.392), channel_id=1, source_target_pairs={{32,0},{40,8},{48,16},{56,24},{64,32},{72,40},{80,48},{88,56},{96,... | collective-permute-start | bytes 196616 | tf_op jit(solution)/shard_map/ppermute | solution.py:18
  400.8 9.0 %collective-permute-start.30 = (f32[2,2,32,128]{3,2,1,0:T(8,128)S(1)}, f32[2,2,32,128]{3,2,1,0:T(8,128)S(1)}, u32[]{:S(2)}, u32[]{:S(2)}) collective-permute-start(f32[2,2,32,128]{3,2,1,0:T(8,128)S(1)} %bitcast.391), channel_id=1, source_target_pairs={{40,0},{48,8},{56,16},{64,24},{72,32},{80,40},{88,48},{96,56},{104... | collective-permute-start | bytes 196616 | tf_op jit(solution)/shard_map/ppermute | solution.py:18
  402.1 12.1 %collective-permute-start.29 = (f32[2,2,32,128]{3,2,1,0:T(8,128)S(1)}, f32[2,2,32,128]{3,2,1,0:T(8,128)S(1)}, u32[]{:S(2)}, u32[]{:S(2)}) collective-permute-start(f32[2,2,32,128]{3,2,1,0:T(8,128)S(1)} %bitcast.390), channel_id=1, source_target_pairs={{48,0},{56,8},{64,16},{72,24},{80,32},{88,40},{96,48},{104,56},{11... | collective-permute-start | bytes 196616 | tf_op jit(solution)/shard_map/ppermute | solution.py:18
  403.4 12.3 %collective-permute-start.28 = (f32[2,2,32,128]{3,2,1,0:T(8,128)S(1)}, f32[2,2,32,128]{3,2,1,0:T(8,128)S(1)}, u32[]{:S(2)}, u32[]{:S(2)}) collective-permute-start(f32[2,2,32,128]{3,2,1,0:T(8,128)S(1)} %bitcast.389), channel_id=1, source_target_pairs={{56,0},{64,8},{72,16},{80,24},{88,32},{96,40},{104,48},{112,56},{1... | collective-permute-start | bytes 196616 | tf_op jit(solution)/shard_map/ppermute | solution.py:18
  497.6 14.6 %all-to-all-start.1 = ((f32[8,2,32,128]{3,2,1,0:T(8,128)}), f32[8,2,32,128]{3,2,1,0:T(8,128)S(1)}, u32[]{:S(2)}, u32[]{:S(2)}) async-start(f32[8,2,32,128]{3,2,1,0:T(8,128)} %stack.175), calls=%async_computation.3 | async-start | bytes 524288 | tf_op jit(solution)/shard_map/all_to_all | solution.py:8
  501.7 137.6 %all-reduce.11.cloned.1.call-start = ((), (), s32[]{:S(2)}) async-start(), calls=%async_computation.8 | async-start | bytes 524288
  513.5 16.8 %collective-permute-start.55 = (f32[1,2,32,128]{3,2,1,0:T(8,128)S(1)}, f32[1,2,32,128]{3,2,1,0:T(8,128)S(1)}, u32[]{:S(2)}, u32[]{:S(2)}) collective-permute-start(f32[1,2,32,128]{3,2,1,0:T(8,128)S(1)} %get-tuple-element.21), channel_id=1, source_target_pairs={{0,56},{8,64},{16,72},{24,80},{32,88},{40,96},{48,104},{56,112},{6... | collective-permute-start | bytes 98312 | tf_op jit(solution)/shard_map/ppermute | solution.py:18
  514.8 19.2 %collective-permute-start.54 = (f32[1,2,32,128]{3,2,1,0:T(8,128)S(1)}, f32[1,2,32,128]{3,2,1,0:T(8,128)S(1)}, u32[]{:S(2)}, u32[]{:S(2)}) collective-permute-start(f32[1,2,32,128]{3,2,1,0:T(8,128)S(1)} %get-tuple-element.22), channel_id=1, source_target_pairs={{0,48},{8,56},{16,64},{24,72},{32,80},{40,88},{48,96},{56,104},{64... | collective-permute-start | bytes 98312 | tf_op jit(solution)/shard_map/ppermute | solution.py:18
  519.0 19.3 %collective-permute-start.53 = (f32[1,2,32,128]{3,2,1,0:T(8,128)S(1)}, f32[1,2,32,128]{3,2,1,0:T(8,128)S(1)}, u32[]{:S(2)}, u32[]{:S(2)}) collective-permute-start(f32[1,2,32,128]{3,2,1,0:T(8,128)S(1)} %get-tuple-element.23), channel_id=1, source_target_pairs={{0,40},{8,48},{16,56},{24,64},{32,72},{40,80},{48,88},{56,96},{64,... | collective-permute-start | bytes 98312 | tf_op jit(solution)/shard_map/ppermute | solution.py:18
  524.4 15.9 %collective-permute-start.52 = (f32[1,2,32,128]{3,2,1,0:T(8,128)S(1)}, f32[1,2,32,128]{3,2,1,0:T(8,128)S(1)}, u32[]{:S(2)}, u32[]{:S(2)}) collective-permute-start(f32[1,2,32,128]{3,2,1,0:T(8,128)S(1)} %get-tuple-element.24), channel_id=1, source_target_pairs={{0,32},{8,40},{16,48},{24,56},{32,64},{40,72},{48,80},{56,88},{64,... | collective-permute-start | bytes 98312 | tf_op jit(solution)/shard_map/ppermute | solution.py:18
  528.5 13.6 %collective-permute-start.51 = (f32[1,2,32,128]{3,2,1,0:T(8,128)S(1)}, f32[1,2,32,128]{3,2,1,0:T(8,128)S(1)}, u32[]{:S(2)}, u32[]{:S(2)}) collective-permute-start(f32[1,2,32,128]{3,2,1,0:T(8,128)S(1)} %get-tuple-element.25), channel_id=1, source_target_pairs={{0,24},{8,32},{16,40},{24,48},{32,56},{40,64},{48,72},{56,80},{64,... | collective-permute-start | bytes 98312 | tf_op jit(solution)/shard_map/ppermute | solution.py:18
  530.3 13.2 %collective-permute-start.50 = (f32[1,2,32,128]{3,2,1,0:T(8,128)S(1)}, f32[1,2,32,128]{3,2,1,0:T(8,128)S(1)}, u32[]{:S(2)}, u32[]{:S(2)}) collective-permute-start(f32[1,2,32,128]{3,2,1,0:T(8,128)S(1)} %get-tuple-element.26), channel_id=1, source_target_pairs={{0,16},{8,24},{16,32},{24,40},{32,48},{40,56},{48,64},{56,72},{64,... | collective-permute-start | bytes 98312 | tf_op jit(solution)/shard_map/ppermute | solution.py:18
  534.0 10.8 %collective-permute-start.49 = (f32[1,2,32,128]{3,2,1,0:T(8,128)S(1)}, f32[1,2,32,128]{3,2,1,0:T(8,128)S(1)}, u32[]{:S(2)}, u32[]{:S(2)}) collective-permute-start(f32[1,2,32,128]{3,2,1,0:T(8,128)S(1)} %get-tuple-element.27), channel_id=1, source_target_pairs={{0,8},{8,16},{16,24},{24,32},{32,40},{40,48},{48,56},{56,64},{64,7... | collective-permute-start | bytes 98312 | tf_op jit(solution)/shard_map/ppermute | solution.py:18
  544.8 8.6 %collective-permute-start.44 = (f32[1,2,32,128]{3,2,1,0:T(8,128)S(1)}, f32[1,2,32,128]{3,2,1,0:T(8,128)S(1)}, u32[]{:S(2)}, u32[]{:S(2)}) collective-permute-start(f32[1,2,32,128]{3,2,1,0:T(8,128)S(1)} %get-tuple-element.32), channel_id=1, source_target_pairs={{40,0},{48,8},{56,16},{64,24},{72,32},{80,40},{88,48},{96,56},{104... | collective-permute-start | bytes 98312 | tf_op jit(solution)/shard_map/ppermute | solution.py:18
  546.1 11.5 %collective-permute-start.43 = (f32[1,2,32,128]{3,2,1,0:T(8,128)S(1)}, f32[1,2,32,128]{3,2,1,0:T(8,128)S(1)}, u32[]{:S(2)}, u32[]{:S(2)}) collective-permute-start(f32[1,2,32,128]{3,2,1,0:T(8,128)S(1)} %get-tuple-element.33), channel_id=1, source_target_pairs={{48,0},{56,8},{64,16},{72,24},{80,32},{88,40},{96,48},{104,56},{11... | collective-permute-start | bytes 98312 | tf_op jit(solution)/shard_map/ppermute | solution.py:18
  547.4 11.6 %collective-permute-start.42 = (f32[1,2,32,128]{3,2,1,0:T(8,128)S(1)}, f32[1,2,32,128]{3,2,1,0:T(8,128)S(1)}, u32[]{:S(2)}, u32[]{:S(2)}) collective-permute-start(f32[1,2,32,128]{3,2,1,0:T(8,128)S(1)} %get-tuple-element.20), channel_id=1, source_target_pairs={{56,0},{64,8},{72,16},{80,24},{88,32},{96,40},{104,48},{112,56},{1... | collective-permute-start | bytes 98312 | tf_op jit(solution)/shard_map/ppermute | solution.py:18
  (21 other events, 352.9 us)
Sparse Core Ops, SparseCore 0:
  85.4 44.6 reduce-scatter.2
  204.2 42.9 reduce-scatter.4
  274.4 76.6 all-reduce.6
  417.2 78.8 all-reduce.8
  560.5 78.7 all-reduce.10
